TPU v7x, 512 devices: a whole 4x8x8 slice. The times are simulated.
512 devices in a mesh: gz: 16 (over y, x_lo), gy: 32 (over x_hi, z, core).
Axes of the slice: x: 4 (x_hi: 2, x_lo: 2; x = x_hi * 2 + x_lo), y: 8, z: 8, core: 2. Of those that a mesh axis runs over, the one named last changes fastest.
Arguments:
- source: bfloat16 [48, 96, 128, 128], P('gz', 'gy'), may hold values from -6 to 6
- target: bfloat16 [48, 96, 128, 128], P('gz', 'gy'), may hold values from -6 to 6
- hidden: bfloat16 [48, 96, 96, 128], P('gz', 'gy'), may hold values from -1 to 1
- motion: float32 [48, 96, 3, 128], P('gz', 'gy'), may hold values from -6 to 6
- w_corr: bfloat16 [96, 343], replicated, may hold values from -0.3125 to 0.3125
- w_motion: float32 [96, 3], replicated, may hold values from -3.5 to 3.5
- bias_encoder: float32 [96], replicated, may hold values from -3 to 3
- w_update: bfloat16 [27, 18432], replicated, may hold values from -0.078125 to 0.078125
- bias_update: float32 [96], replicated, may hold values from -4 to 4
- w_reset: bfloat16 [27, 18432], replicated, may hold values from -0.078125 to 0.078125
- bias_reset: float32 [96], replicated, may hold values from -4 to 4
- w_cand: bfloat16 [27, 18432], replicated, may hold values from -0.078125 to 0.078125
- bias_cand: float32 [96], replicated, may hold values from -3 to 3
- w_head: bfloat16 [27, 3, 96], replicated, may hold values from -0.125 to 0.125
- bias_head: float32 [3], replicated, may hold values from -3 to 3
Outputs:
- state_out: bfloat16 [48, 96, 96, 128], P('gz', 'gy')
- motion_out: float32 [48, 96, 3, 128], P('gz', 'gy')
All inputs are finite; a program needn't handle non-finite values.
Results may differ from a plain program's by a relative error of at most 0.0046.
Values may be sent and summed in bfloat16 or wider, within the bound.
A program may use at most 64 MiB of HBM per device.

v0:
```python
import functools

import jax
import jax.numpy as jnp
from jax import lax
from jax.experimental import pallas as pl
from jax.experimental.pallas import tpu as pltpu
from jax.sharding import PartitionSpec as P

MESH = pl.DeviceIdType.MESH
F32 = jnp.float32
BF16 = jnp.bfloat16
DIRS = [(dz, dy) for dz in (-1, 0, 1) for dy in (-1, 0, 1) if (dz, dy) != (0, 0)]


def iota(shape, dim):
    return lax.broadcasted_iota(jnp.int32, shape, dim)


def kernel(nz, ny,
           src_hbm, tgt_hbm, hid_hbm, motion, w_corr, w_motion, b_enc, w_upd, b_upd, w_res, b_res, w_cand, b_cand, w_head, b_head,
           state_out, motion_out,
           src, text, hext, eext, gext, sext, wraw, tmp_h, tmp_e, wh, we, wc, whead, headtmp, st, corr, ph, pe,
           loc_sem, blk_send, blk_recv, rim_send, rim_recv):
    gz = lax.axis_index("gz")
    gy = lax.axis_index("gy")
    odd = gz % 2
    s = 1 - 2 * odd
    has_relay_dst = (gz + 2 * s >= 0) & (gz + 2 * s < nz)
    has_relay = (gz - s >= 0) & (gz - s < nz)
    part_plane = 3 + 3 * s
    relay_plane = 3 - 3 * s

    local = []

    def fetch(a, b):
        c = pltpu.make_async_copy(a, b, loc_sem.at[len(local)])
        c.start()
        local.append(c)

    fetch(tgt_hbm, text.at[pl.ds(3, 3), pl.ds(3, 3)])
    fetch(src_hbm, src)
    fetch(hid_hbm, hext.at[pl.ds(1, 3), pl.ds(1, 3)])
    fetch(w_res, wraw.at[0])
    fetch(w_upd, wraw.at[1])
    fetch(w_cand, wraw.at[2])

    barrier = pltpu.get_barrier_semaphore()

    def exists(dz, dy):
        ok = (gz + dz >= 0) & (gz + dz < nz)
        return ok & (gy + dy >= 0) & (gy + dy < ny)

    others = DIRS + [(-2, 0), (2, 0)]
    for dz, dy in others:
        @pl.when(exists(dz, dy))
        def _():
            pl.semaphore_signal(barrier, inc=1, device_id=(gz + dz, gy + dy), device_id_type=MESH)

    for cond, at in (
        (gz == 0, (0, None)), (gz == nz - 1, (1, None)), (gy == 0, (None, 0)), (gy == ny - 1, (None, 1)),
    ):
        @pl.when(cond)
        def _():
            if at[0] is not None:
                def zp(i, c):
                    text[6 * at[0] + i // 9, i % 9] = jnp.zeros((128, 128), BF16)
                    return c
                lax.fori_loop(0, 27, zp, 0)
                for e in (hext, eext, gext, sext):
                    def ze(i, c):
                        e[4 * at[0], i] = jnp.zeros((96, 128), BF16)
                        return c
                    lax.fori_loop(0, 5, ze, 0)
            else:
                def zp(i, c):
                    text[i // 3, 6 * at[1] + i % 3] = jnp.zeros((128, 128), BF16)
                    return c
                lax.fori_loop(0, 27, zp, 0)
                for e in (hext, eext, gext, sext):
                    def ze(i, c):
                        e[i, 4 * at[1]] = jnp.zeros((96, 128), BF16)
                        return c
                    lax.fori_loop(0, 5, ze, 0)

    local[0].wait()
    local[2].wait()
    zs = sum((d + nz - 1) // nz for d in (gz, nz - 1 - gz))
    ys = sum((d + ny - 1) // ny for d in (gy, ny - 1 - gy))
    zs2 = sum((d + nz - 2) // nz for d in (gz, nz - 1 - gz))
    pl.semaphore_wait(barrier, (1 + zs) * (1 + ys) - 1 + zs2)

    def partner_copy(k):
        return pltpu.make_async_remote_copy(
            src_ref=text.at[3 + k, pl.ds(3, 3)], dst_ref=text.at[relay_plane + k, pl.ds(3, 3)],
            send_sem=blk_send.at[k], recv_sem=blk_recv.at[k],
            device_id=(gz + s, gy), device_id_type=MESH)

    def relay_copy(k):
        return pltpu.make_async_remote_copy(
            src_ref=text.at[part_plane + k, pl.ds(3, 3)], dst_ref=text.at[relay_plane + k, pl.ds(3, 3)],
            send_sem=blk_send.at[3 + k], recv_sem=blk_recv.at[3 + k],
            device_id=(gz + 2 * s, gy), device_id_type=MESH)

    def row_copy(group, k, side):
        plane = (3, part_plane, relay_plane)[group] + k
        i = 6 + (group * 3 + k) * 2 + side
        return pltpu.make_async_remote_copy(
            src_ref=text.at[plane, pl.ds(3, 3)], dst_ref=text.at[plane, pl.ds(6 - 6 * side, 3)],
            send_sem=blk_send.at[i], recv_sem=blk_recv.at[i],
            device_id=(gz, gy + 2 * side - 1), device_id_type=MESH)

    side_ok = (gy > 0, gy < ny - 1)

    def rows_start(group, k):
        for side in (0, 1):
            @pl.when(side_ok[side])
            def _():
                row_copy(group, k, side).start()

    def rows_recv(group, k):
        for side in (0, 1):
            @pl.when(side_ok[1 - side])
            def _():
                row_copy(group, k, side).wait_recv()

    def rows_sent(group, k):
        for side in (0, 1):
            @pl.when(side_ok[side])
            def _():
                row_copy(group, k, side).wait_send()

    for k in range(3):
        partner_copy(k).start()
        rows_start(0, k)

    def rim_copy(rnd, ref, d):
        dz, dy = DIRS[d]

        def sl(o, here):
            if o == 0:
                return pl.ds(1, 3)
            return pl.ds((3 if o > 0 else 1) if here else (0 if o > 0 else 4), 1)
        return pltpu.make_async_remote_copy(
            src_ref=ref.at[sl(dz, True), sl(dy, True)], dst_ref=ref.at[sl(dz, False), sl(dy, False)],
            send_sem=rim_send.at[rnd * 8 + d], recv_sem=rim_recv.at[rnd * 8 + d],
            device_id=(gz + dz, gy + dy), device_id_type=MESH)

    def rim_start(rnd, ref):
        for d, (dz, dy) in enumerate(DIRS):
            @pl.when(exists(dz, dy))
            def _():
                rim_copy(rnd, ref, d).start()

    def rim_recv_all(rnd, ref):
        for d, (dz, dy) in enumerate(DIRS):
            @pl.when(exists(-dz, -dy))
            def _():
                rim_copy(rnd, ref, d).wait_recv()

    def rim_sent(rnd, ref):
        for d, (dz, dy) in enumerate(DIRS):
            @pl.when(exists(dz, dy))
            def _():
                rim_copy(rnd, ref, d).wait_send()

    rim_start(0, hext)

    lane8 = iota((8, 128), 1)
    row8 = iota((8, 128), 0)
    flip = jnp.where(iota((128, 128), 0) + iota((128, 128), 1) == 127, 1.0, 0.0).astype(BF16)

    for a in range(7):
        kk = iota((343, 128), 1)
        want = a * 49 + (kk // 8) * 7 + kk % 8
        pick = (iota((343, 128), 0) == want) & (kk % 8 < 7) & (kk < 56)
        wc[:, a * 128:(a + 1) * 128] = jnp.dot(
            w_corr[...], jnp.where(pick, 1.0, 0.0).astype(BF16), preferred_element_type=F32).astype(BF16)

    local[1].wait()

    def turn(p, c):
        st[p] = lax.dot_general(
            flip, src[p // 3, p % 3], (((1,), (1,)), ((), ())), preferred_element_type=F32).astype(BF16)
        return c
    lax.fori_loop(0, 9, turn, 0)

    headtmp[...] = jnp.zeros_like(headtmp)
    for ab in range(9):
        for c in range(3):
            headtmp[c * 8:c * 8 + 3, ab * 96:(ab + 1) * 96] = w_head[ab * 3 + c].astype(F32)
    whead[...] = headtmp[...].astype(BF16)

    for c in local[3:]:
        c.wait()

    def prep(w, carry):
        def spread(op, c):
            x = wraw[w, :, pl.ds(pl.multiple_of(op * 384, 384), 384)].astype(F32)
            r = pl.multiple_of(op * 64, 64)
            tmp_h[pl.ds(r, 27), 0:96] = x[:, 0:96]
            tmp_e[pl.ds(r, 27), 0:96] = x[:, 96:192]
            tmp_h[pl.ds(r + 32, 27), 0:96] = x[:, 192:288]
            tmp_e[pl.ds(r + 32, 27), 0:96] = x[:, 288:384]
            return c
        lax.fori_loop(0, 48, spread, 0)
        for tmp, dst in ((tmp_h, wh), (tmp_e, we)):
            for ab in range(9):
                for c in range(3):
                    v = tmp[pl.ds(ab * 3 + c, 96, stride=32), :]
                    dst[pl.ds(pl.multiple_of(w * 288 + c * 96, 96), 96), ab * 96:(ab + 1) * 96] = v[:, 0:96].astype(BF16)

        @pl.when(w == 0)
        def _():
            for k in range(3):
                partner_copy(k).wait_recv()

                @pl.when(has_relay_dst)
                def _():
                    relay_copy(k).start()
                rows_start(1, k)

        @pl.when((w == 1) & has_relay)
        def _():
            for k in range(3):
                relay_copy(k).wait_recv()
                rows_start(2, k)
        return carry
    lax.fori_loop(0, 3, prep, 0)

    half = lane8 < 64

    def corr_tile(z, y, zt):
        p = z * 3 + y
        lhs = st[p]
        mixed = []
        for b in range(7):
            g = jnp.dot(lhs, text[zt, y + b], preferred_element_type=F32)
            skewed = []
            for par in range(2):
                v = g[8 * par:8 * par + 8]
                for r in range(par + 2, 16, 2):
                    v = jnp.where(lane8 < 132 - 8 * r, g[8 * r:8 * r + 8], v)
                skewed.append(pltpu.roll(v, 4, 1, stride=1, stride_axis=0))
            mixed.append(jnp.where((lane8 & 8) == 0, skewed[0], skewed[1]))
        mixed.append(jnp.zeros((8, 128), F32))
        for d in (1, 2, 4):
            new = list(mixed)
            keep = (lane8 & (8 * d)) == 0
            for i in range(8):
                if not i & d:
                    lo, hi = mixed[i], mixed[i + d]
                    new[i] = jnp.where(keep, lo, pltpu.roll(hi, 8 * d, 1))
                    new[i + d] = jnp.where(keep, pltpu.roll(lo, 128 - 8 * d, 1), hi)
            mixed = new
        rows = []
        for r in range(16):
            group = (16 - r) % 16
            v = mixed[group % 8]
            if group >= 8:
                v = pltpu.roll(v, 64, 1)
            keep = half
            if r in (0, 15):
                xt = 127 - 8 * r - row8 + (lane8 & 7) - 3
                keep = keep & (xt >= 0) & (xt < 128)
            rows.append(jnp.where(keep, v, 0.0))
        tile = (jnp.concatenate(rows, axis=0) * (128.0 ** -0.5)).astype(BF16)
        corr[p * 7 + zt - z] = tile

    for k in range(3):
        rows_recv(0, k)

    def own(i, c):
        corr_tile(i // 9, i // 3 % 3, 3 + i % 3)
        return c
    lax.fori_loop(0, 27, own, 0)

    for k in range(3):
        rows_recv(1, k)

    @pl.when(has_relay)
    def _():
        for k in range(3):
            rows_recv(2, k)

    def outer(up, k, i):
        z, zt = k + i // 3, 6 + k
        corr_tile((1 - up) * (2 - z) + up * z, i % 3, (1 - up) * (8 - zt) + up * zt)

    for k in range(3):
        def both(i, c):
            n = 3 * (3 - k)
            outer(i // n, k, i % n)
            return c
        lax.fori_loop(0, 6 * (3 - k), both, 0)

    back = 127 - iota((8, 128), 1)

    def encode(p, carry):
        z, y = p // 3, p % 3
        acc = jnp.zeros((96, 128), F32)
        for a in range(7):
            acc = acc + lax.dot_general(
                wc[:, a * 128:(a + 1) * 128], corr[p * 7 + a], (((1,), (1,)), ((), ())), preferred_element_type=F32)
        m = motion[z, y]
        term = jnp.zeros((96, 128), F32)
        for j in range(3):
            mj = jnp.broadcast_to(m[j:j + 1], (8, 128))
            mj = jnp.take_along_axis(mj, back, axis=1, mode="promise_in_bounds")
            term = term + w_motion[:, j:j + 1] * jnp.concatenate([mj] * 12, axis=0)
        e = jnp.maximum(acc + term + b_enc[...], 0.0).astype(BF16)
        eext[1 + z, 1 + y] = jnp.dot(e, flip, preferred_element_type=F32).astype(BF16)
        return carry
    lax.fori_loop(0, 9, encode, 0)
    rim_start(1, eext)

    def field(ref):
        cols = []
        for p in range(9):
            z, y = p // 3, p % 3
            cols.append(jnp.concatenate([ref[z + a, y + b] for a in range(3) for b in range(3)], axis=0))
        return jnp.concatenate(cols, axis=1)

    def shifted(parts, p):
        lane = iota((parts[0].shape[0], 128), 1)
        cut = slice(p * 128, (p + 1) * 128)
        left = jnp.where(lane == 0, 0.0, pltpu.roll(parts[0][:, cut], 1, 1))
        right = jnp.where(lane == 127, 0.0, pltpu.roll(parts[2][:, cut], 127, 1))
        return left + parts[1][:, cut] + right

    rim_recv_all(0, hext)
    ph[...] = jnp.dot(wh[0:576], field(hext), preferred_element_type=F32)
    rim_recv_all(1, eext)
    pe[0:288] = jnp.dot(we[0:288], field(eext), preferred_element_type=F32) + ph[0:288]

    def pick(ref, base):
        return [ref[base + c * 96:base + (c + 1) * 96] for c in range(3)]

    for p in range(9):
        z, y = p // 3, p % 3
        r = jax.nn.sigmoid(shifted(pick(pe, 0), p) + b_res[...])
        gext[1 + z, 1 + y] = (r * hext[1 + z, 1 + y].astype(F32)).astype(BF16)
    rim_start(2, gext)

    pe[288:864] = jnp.dot(we[288:864], field(eext), preferred_element_type=F32)
    for c in range(3):
        ph[288 + c * 96:288 + (c + 1) * 96] += pe[288 + c * 96:288 + (c + 1) * 96]
    for p in range(9):
        ph[0:96, p * 128:(p + 1) * 128] = jax.nn.sigmoid(shifted(pick(ph, 288), p) + b_upd[...])
    rim_recv_all(2, gext)
    pe[0:288] = jnp.dot(wh[576:864], field(gext), preferred_element_type=F32) + pe[576:864]
    for p in range(9):
        z, y = p // 3, p % 3
        cand = jnp.tanh(shifted(pick(pe, 0), p) + b_cand[...])
        u = ph[0:96, p * 128:(p + 1) * 128]
        new = ((1.0 - u) * hext[1 + z, 1 + y].astype(F32) + u * cand).astype(BF16)
        sext[1 + z, 1 + y] = new
        state_out[z, y] = new
    rim_start(3, sext)
    rim_recv_all(3, sext)
    pe[0:24] = jnp.dot(whead[...], field(sext), preferred_element_type=F32)
    for p in range(9):
        z, y = p // 3, p % 3
        out = shifted([pe[c * 8:(c + 1) * 8] for c in range(3)], p)
        motion_out[z, y] = motion[z, y] + out[0:3] + b_head[...]

    for k in range(3):
        partner_copy(k).wait_send()

        @pl.when(has_relay_dst)
        def _():
            relay_copy(k).wait_send()
        rows_sent(0, k)
        rows_sent(1, k)

        @pl.when(has_relay)
        def _():
            rows_sent(2, k)
    for rnd, ref in enumerate((hext, eext, gext, sext)):
        rim_sent(rnd, ref)


def solution(mesh):
    nz, ny = mesh.shape["gz"], mesh.shape["gy"]

    def on_device(source, target, hidden, motion, w_corr, w_motion, bias_encoder, w_update, bias_update, w_reset, bias_reset,
                  w_cand, bias_cand, w_head, bias_head):
        hbm = pl.BlockSpec(memory_space=pl.ANY)
        vmem = pl.BlockSpec(memory_space=pltpu.VMEM)
        ext = pltpu.VMEM((5, 5, 96, 128), BF16)
        return pl.pallas_call(
            functools.partial(kernel, nz, ny),
            name="dvc_update",
            out_shape=(jax.ShapeDtypeStruct((3, 3, 96, 128), BF16), jax.ShapeDtypeStruct((3, 3, 3, 128), F32)),
            in_specs=[hbm, hbm, hbm, vmem, vmem, vmem, vmem, hbm, vmem, hbm, vmem, hbm, vmem, vmem, vmem],
            out_specs=(vmem, vmem),
            scratch_shapes=[
                pltpu.VMEM((3, 3, 128, 128), BF16),
                pltpu.VMEM((9, 9, 128, 128), BF16),
                ext, ext, ext, ext,
                pltpu.VMEM((3, 27, 18432), BF16),
                pltpu.VMEM((3072, 128), F32), pltpu.VMEM((3072, 128), F32),
                pltpu.VMEM((864, 864), BF16), pltpu.VMEM((864, 864), BF16),
                pltpu.VMEM((96, 896), BF16),
                pltpu.VMEM((24, 864), BF16), pltpu.VMEM((24, 864), F32),
                pltpu.VMEM((9, 128, 128), BF16),
                pltpu.VMEM((63, 128, 128), BF16),
                pltpu.VMEM((576, 1152), F32),
                pltpu.VMEM((864, 1152), F32),
                pltpu.SemaphoreType.DMA((6,)),
                pltpu.SemaphoreType.DMA((24,)), pltpu.SemaphoreType.DMA((24,)),
                pltpu.SemaphoreType.DMA((32,)), pltpu.SemaphoreType.DMA((32,)),
            ],
            compiler_params=pltpu.CompilerParams(
                collective_id=0, has_side_effects=True, vmem_limit_bytes=60 * 2 ** 20),
        )(source, target, hidden, motion, w_corr, w_motion, bias_encoder[:, None], w_update, bias_update[:, None], w_reset,
          bias_reset[:, None], w_cand, bias_cand[:, None], w_head, bias_head[:, None])

    rows = P("gz", "gy", None, None)
    return jax.shard_map(
        on_device, mesh=mesh, in_specs=(rows,) * 4 + (P(),) * 11, out_specs=(rows, rows), check_vma=False)
```

profile of v0, /device:TPU:463, one launch (start us, length us, event | category | flops | bytes accessed | tf_op | source)
XLA Modules:
  0.0 112.6 jit_solution(1129805127105753950)
XLA Ops:
  0.6 1.3 %copy.23.b_head = f32[3,1]{1,0:T(4,128)} copy(f32[3,1]{0,1:T(1,128)} %bitcast.9) | data formatting | bytes 24 | tf_op jit(solution)/shard_map/broadcast_in_dim | solution.py:417
  1.9 1.4 %copy.22.w_head = bf16[27,3,96]{2,1,0:T(4,128)(2,1)} copy(bf16[27,3,96]{2,0,1:T(8,128)(2,1)} %param.28) | data formatting | bytes 31104 | tf_op args[13]
  3.3 1.4 %copy.17.w_motion = f32[96,3]{1,0:T(8,128)} copy(f32[96,3]{0,1:T(4,128)} %param.20) | data formatting | bytes 2304 | tf_op args[5]
  4.7 1.4 %copy.18.b_enc = f32[96,1]{1,0:T(8,128)} copy(f32[96,1]{0,1:T(1,128)} %bitcast.5) | data formatting | bytes 768 | tf_op jit(solution)/shard_map/broadcast_in_dim | solution.py:416
  6.1 1.4 %copy.19.b_upd = f32[96,1]{1,0:T(8,128)} copy(f32[96,1]{0,1:T(1,128)} %bitcast.6) | data formatting | bytes 768 | tf_op jit(solution)/shard_map/broadcast_in_dim | solution.py:416
  7.4 1.4 %copy.20.b_res = f32[96,1]{1,0:T(8,128)} copy(f32[96,1]{0,1:T(1,128)} %bitcast.7) | data formatting | bytes 768 | tf_op jit(solution)/shard_map/broadcast_in_dim | solution.py:417
  8.8 1.4 %copy.21.b_cand = f32[96,1]{1,0:T(8,128)} copy(f32[96,1]{0,1:T(1,128)} %bitcast.8) | data formatting | bytes 768 | tf_op jit(solution)/shard_map/broadcast_in_dim | solution.py:417
  10.2 99.4 %dvc_update.1 = (bf16[3,3,96,128]{3,2,1,0:T(8,128)(2,1)}, f32[3,3,3,128]{3,2,1,0:T(4,128)}) custom-call(bf16[3,3,128,128]{3,2,1,0:T(8,128)(2,1)} %src_hbm.1, bf16[3,3,128,128]{3,2,1,0:T(8,128)(2,1)} %tgt_hbm.1, bf16[3,3,96,128]{3,2,1,0:T(8,128)(2,1)} %hid_hbm.1, f32[3,3,3,128]{3,2,1,0:T(4,128)} %motion.1, bf16[96,343]{1,0:T(8,128)(2,1)} %w_corr.1, ...), custom_call_target="tpu_custom_call" | custom-call | tf_op jit(solution)/shard_map/dvc_update/pallas_call | solution.py:391
  109.6 1.6 %copy.26 = bf16[3,3,96,128]{3,2,1,0:T(8,128)(2,1)} copy(bf16[3,3,96,128]{3,2,1,0:T(8,128)(2,1)} %get-tuple-element.4) | data formatting | bytes 442368
  111.2 1.3 %copy.27 = f32[3,3,3,128]{3,2,1,0:T(4,128)} copy(f32[3,3,3,128]{3,2,1,0:T(4,128)} %get-tuple-element.5) | data formatting | bytes 27648
where the time goes:
time: 113 us
  Pallas kernels  99.4 us (88%)
  local copies, waits for them, and re-layouts  12.5 us (11%)
    pallas_call x1, Pallas kernels, on_device(): pl.pallas_call(functools.partial(kernel, nz, ny), name='dvc_update', out_...  99.4 us
    unnamed x4, local copies, waits for them, and re-layouts  5.73 us

commit v1 on v0

--- a/solution.py
+++ b/solution.py
@@ -10,6 +10,7 @@
 MESH = pl.DeviceIdType.MESH
 F32 = jnp.float32
 BF16 = jnp.bfloat16
+GROUPS = ((0, 1), (2, 3), (4, 5), (6, 7), (8,))
 DIRS = [(dz, dy) for dz in (-1, 0, 1) for dy in (-1, 0, 1) if (dz, dy) != (0, 0)]
 
 
@@ -164,8 +165,6 @@
             def _():
                 rim_copy(rnd, ref, d).wait_send()
 
-    rim_start(0, hext)
-
     lane8 = iota((8, 128), 1)
     row8 = iota((8, 128), 0)
     flip = jnp.where(iota((128, 128), 0) + iota((128, 128), 1) == 127, 1.0, 0.0).astype(BF16)
@@ -179,139 +178,166 @@
 
     local[1].wait()
 
-    def turn(p, c):
-        st[p] = lax.dot_general(
+    for p in range(9):
+        st[p * 128:(p + 1) * 128] = lax.dot_general(
             flip, src[p // 3, p % 3], (((1,), (1,)), ((), ())), preferred_element_type=F32).astype(BF16)
-        return c
-    lax.fori_loop(0, 9, turn, 0)
 
     headtmp[...] = jnp.zeros_like(headtmp)
-    for ab in range(9):
-        for c in range(3):
-            headtmp[c * 8:c * 8 + 3, ab * 96:(ab + 1) * 96] = w_head[ab * 3 + c].astype(F32)
+    for o in range(3):
+        v = w_head[o].astype(F32)
+        for ab in range(9):
+            for c in range(3):
+                headtmp[c * 8 + o:c * 8 + o + 1, ab * 96:(ab + 1) * 96] = v[ab * 3 + c:ab * 3 + c + 1]
     whead[...] = headtmp[...].astype(BF16)
 
-    for c in local[3:]:
-        c.wait()
-
-    def prep(w, carry):
-        def spread(op, c):
-            x = wraw[w, :, pl.ds(pl.multiple_of(op * 384, 384), 384)].astype(F32)
-            r = pl.multiple_of(op * 64, 64)
-            tmp_h[pl.ds(r, 27), 0:96] = x[:, 0:96]
-            tmp_e[pl.ds(r, 27), 0:96] = x[:, 96:192]
-            tmp_h[pl.ds(r + 32, 27), 0:96] = x[:, 192:288]
-            tmp_e[pl.ds(r + 32, 27), 0:96] = x[:, 288:384]
+    def spread(w):
+        local[3 + w].wait()
+
+        def some(op4, c):
+            for u in range(4):
+                op = op4 * 4 + u
+                x = wraw[w, :, pl.ds(pl.multiple_of(op * 384, 384), 384)].astype(F32)
+                r = pl.multiple_of(op * 64, 64)
+                tmp_h[pl.ds(r, 27), 0:96] = x[:, 0:96]
+                tmp_e[pl.ds(r, 27), 0:96] = x[:, 96:192]
+                tmp_h[pl.ds(r + 32, 27), 0:96] = x[:, 192:288]
+                tmp_e[pl.ds(r + 32, 27), 0:96] = x[:, 288:384]
             return c
-        lax.fori_loop(0, 48, spread, 0)
+        lax.fori_loop(0, 12, some, 0)
+
+    def collect(w):
         for tmp, dst in ((tmp_h, wh), (tmp_e, we)):
             for ab in range(9):
                 for c in range(3):
                     v = tmp[pl.ds(ab * 3 + c, 96, stride=32), :]
-                    dst[pl.ds(pl.multiple_of(w * 288 + c * 96, 96), 96), ab * 96:(ab + 1) * 96] = v[:, 0:96].astype(BF16)
-
-        @pl.when(w == 0)
-        def _():
-            for k in range(3):
-                partner_copy(k).wait_recv()
-
-                @pl.when(has_relay_dst)
-                def _():
-                    relay_copy(k).start()
-                rows_start(1, k)
-
-        @pl.when((w == 1) & has_relay)
-        def _():
-            for k in range(3):
-                relay_copy(k).wait_recv()
-                rows_start(2, k)
-        return carry
-    lax.fori_loop(0, 3, prep, 0)
+                    row = w * 288 + c * 96
+                    dst[row:row + 96, ab * 96:(ab + 1) * 96] = v[:, 0:96].astype(BF16)
+
+    def pass_partner(k):
+        partner_copy(k).wait_recv()
+
+        @pl.when(has_relay_dst)
+        def _():
+            relay_copy(k).start()
+        rows_start(1, k)
+
+    def pass_relay(k):
+        @pl.when(has_relay)
+        def _():
+            relay_copy(k).wait_recv()
+            rows_start(2, k)
+
+    pass_partner(0)
+    spread(0)
+    pass_partner(1)
+    collect(0)
+    pass_partner(2)
 
     half = lane8 < 64
 
-    def corr_tile(z, y, zt):
-        p = z * 3 + y
-        lhs = st[p]
-        mixed = []
-        for b in range(7):
-            g = jnp.dot(lhs, text[zt, y + b], preferred_element_type=F32)
+    def corr_rows(z, zt):
+        mixed = [[None] * 8 for _ in range(3)]
+
+        def diagonals(g):
             skewed = []
             for par in range(2):
-                v = g[8 * par:8 * par + 8]
+                v = g(par)
                 for r in range(par + 2, 16, 2):
-                    v = jnp.where(lane8 < 132 - 8 * r, g[8 * r:8 * r + 8], v)
+                    v = jnp.where(lane8 < 132 - 8 * r, g(r), v)
                 skewed.append(pltpu.roll(v, 4, 1, stride=1, stride_axis=0))
-            mixed.append(jnp.where((lane8 & 8) == 0, skewed[0], skewed[1]))
-        mixed.append(jnp.zeros((8, 128), F32))
-        for d in (1, 2, 4):
-            new = list(mixed)
-            keep = (lane8 & (8 * d)) == 0
-            for i in range(8):
-                if not i & d:
-                    lo, hi = mixed[i], mixed[i + d]
-                    new[i] = jnp.where(keep, lo, pltpu.roll(hi, 8 * d, 1))
-                    new[i + d] = jnp.where(keep, pltpu.roll(lo, 128 - 8 * d, 1), hi)
-            mixed = new
-        rows = []
-        for r in range(16):
-            group = (16 - r) % 16
-            v = mixed[group % 8]
-            if group >= 8:
-                v = pltpu.roll(v, 64, 1)
-            keep = half
-            if r in (0, 15):
-                xt = 127 - 8 * r - row8 + (lane8 & 7) - 3
-                keep = keep & (xt >= 0) & (xt < 128)
-            rows.append(jnp.where(keep, v, 0.0))
-        tile = (jnp.concatenate(rows, axis=0) * (128.0 ** -0.5)).astype(BF16)
-        corr[p * 7 + zt - z] = tile
+            return jnp.where((lane8 & 8) == 0, skewed[0], skewed[1])
+
+        for group in GROUPS:
+            lo = max(0, min(group) - 6)
+            hi = min(2, max(group))
+            lhs = st[pl.ds(pl.multiple_of((z * 3 + lo) * 128, 128), (hi - lo + 1) * 128)]
+            rhs = jnp.concatenate([text[zt, row] for row in group], axis=1)
+            g = jnp.dot(lhs, rhs, preferred_element_type=F32)
+            for n, row in enumerate(group):
+                for y in range(lo, hi + 1):
+                    if 0 <= row - y <= 6:
+                        mixed[y][row - y] = diagonals(
+                            lambda r: g[(y - lo) * 128 + 8 * r:(y - lo) * 128 + 8 * r + 8, n * 128:(n + 1) * 128])
+        for y in range(3):
+            mix = mixed[y]
+            mix[7] = jnp.zeros((8, 128), F32)
+            for d in (1, 2, 4):
+                new = list(mix)
+                keep = (lane8 & (8 * d)) == 0
+                for i in range(8):
+                    if not i & d:
+                        a, b = mix[i], mix[i + d]
+                        new[i] = jnp.where(keep, a, pltpu.roll(b, 8 * d, 1))
+                        new[i + d] = jnp.where(keep, pltpu.roll(a, 128 - 8 * d, 1), b)
+                mix = new
+            rows = []
+            for r in range(16):
+                at = (16 - r) % 16
+                v = mix[at % 8]
+                if at >= 8:
+                    v = pltpu.roll(v, 64, 1)
+                keep = half
+                if r in (0, 15):
+                    xt = 127 - 8 * r - row8 + (lane8 & 7) - 3
+                    keep = keep & (xt >= 0) & (xt < 128)
+                rows.append(jnp.where(keep, v, 0.0))
+            tile = (jnp.concatenate(rows, axis=0) * (128.0 ** -0.5)).astype(BF16)
+            corr[pl.ds(pl.multiple_of((z * 3 + y) * 128, 128), 128), pl.ds(pl.multiple_of((zt - z) * 128, 128), 128)] = tile
 
     for k in range(3):
         rows_recv(0, k)
 
     def own(i, c):
-        corr_tile(i // 9, i // 3 % 3, 3 + i % 3)
+        corr_rows(i // 3, 3 + i % 3)
+        for at, k in ((0, 0), (1, 1), (3, 2)):
+            @pl.when(i == at)
+            def _():
+                pass_relay(k)
         return c
-    lax.fori_loop(0, 27, own, 0)
-
-    for k in range(3):
-        rows_recv(1, k)
-
-    @pl.when(has_relay)
-    def _():
+    lax.fori_loop(0, 9, own, 0)
+    rim_start(0, hext)
+
+    def side(n, carry):
+        up = (1 - odd) * (1 - n) + odd * n
+
+        @pl.when(n == 0)
+        def _():
+            for k in range(3):
+                rows_recv(1, k)
+
+        @pl.when((n == 1) & has_relay)
+        def _():
+            for k in range(3):
+                rows_recv(2, k)
         for k in range(3):
-            rows_recv(2, k)
-
-    def outer(up, k, i):
-        z, zt = k + i // 3, 6 + k
-        corr_tile((1 - up) * (2 - z) + up * z, i % 3, (1 - up) * (8 - zt) + up * zt)
-
-    for k in range(3):
-        def both(i, c):
-            n = 3 * (3 - k)
-            outer(i // n, k, i % n)
-            return c
-        lax.fori_loop(0, 6 * (3 - k), both, 0)
-
-    back = 127 - iota((8, 128), 1)
-
-    def encode(p, carry):
-        z, y = p // 3, p % 3
-        acc = jnp.zeros((96, 128), F32)
-        for a in range(7):
-            acc = acc + lax.dot_general(
-                wc[:, a * 128:(a + 1) * 128], corr[p * 7 + a], (((1,), (1,)), ((), ())), preferred_element_type=F32)
-        m = motion[z, y]
-        term = jnp.zeros((96, 128), F32)
+            def cell(z, c):
+                zt = 6 + k
+                corr_rows((1 - up) * (2 - z) + up * z, (1 - up) * (8 - zt) + up * zt)
+                return c
+            lax.fori_loop(k, 3, cell, 0)
+        return carry
+    lax.fori_loop(0, 2, side, 0)
+
+    eye = iota((96, 96), 0) == iota((96, 96), 1)
+
+    def column(row):
+        return jnp.sum(jnp.where(eye, jnp.broadcast_to(row, (96, 96)), 0.0), axis=1, keepdims=True)
+
+    pe[0:96] = lax.dot_general(wc[...], corr[...], (((1,), (1,)), ((), ())), preferred_element_type=F32)
+    back = 127 - lane8
+    enc_bias = jnp.broadcast_to(column(b_enc[...]), (96, 128))
+    enc_motion = [jnp.broadcast_to(column(w_motion[j:j + 1]), (96, 128)) for j in range(3)]
+    turned = []
+    for p in range(9):
+        m = motion[p // 3, p % 3]
+        e = pe[0:96, p * 128:(p + 1) * 128] + enc_bias
         for j in range(3):
-            mj = jnp.broadcast_to(m[j:j + 1], (8, 128))
-            mj = jnp.take_along_axis(mj, back, axis=1, mode="promise_in_bounds")
-            term = term + w_motion[:, j:j + 1] * jnp.concatenate([mj] * 12, axis=0)
-        e = jnp.maximum(acc + term + b_enc[...], 0.0).astype(BF16)
-        eext[1 + z, 1 + y] = jnp.dot(e, flip, preferred_element_type=F32).astype(BF16)
-        return carry
-    lax.fori_loop(0, 9, encode, 0)
+            mj = jnp.take_along_axis(jnp.broadcast_to(m[j:j + 1], (8, 128)), back, axis=1, mode="promise_in_bounds")
+            e = e + enc_motion[j] * jnp.concatenate([mj] * 12, axis=0)
+        turned.append(jnp.maximum(e, 0.0).astype(BF16))
+    straight = jnp.dot(jnp.concatenate(turned, axis=0), flip, preferred_element_type=F32).astype(BF16)
+    for p in range(9):
+        eext[1 + p // 3, 1 + p % 3] = straight[p * 96:(p + 1) * 96]
     rim_start(1, eext)
 
     def field(ref):
@@ -328,6 +354,8 @@
         right = jnp.where(lane == 127, 0.0, pltpu.roll(parts[2][:, cut], 127, 1))
         return left + parts[1][:, cut] + right
 
+    spread(1)
+    collect(1)
     rim_recv_all(0, hext)
     ph[...] = jnp.dot(wh[0:576], field(hext), preferred_element_type=F32)
     rim_recv_all(1, eext)
@@ -336,22 +364,27 @@
     def pick(ref, base):
         return [ref[base + c * 96:base + (c + 1) * 96] for c in range(3)]
 
+    res_bias = column(b_res[...])
     for p in range(9):
         z, y = p // 3, p % 3
-        r = jax.nn.sigmoid(shifted(pick(pe, 0), p) + b_res[...])
+        r = jax.nn.sigmoid(shifted(pick(pe, 0), p) + res_bias)
         gext[1 + z, 1 + y] = (r * hext[1 + z, 1 + y].astype(F32)).astype(BF16)
     rim_start(2, gext)
+    spread(2)
+    collect(2)
 
     pe[288:864] = jnp.dot(we[288:864], field(eext), preferred_element_type=F32)
     for c in range(3):
         ph[288 + c * 96:288 + (c + 1) * 96] += pe[288 + c * 96:288 + (c + 1) * 96]
-    for p in range(9):
-        ph[0:96, p * 128:(p + 1) * 128] = jax.nn.sigmoid(shifted(pick(ph, 288), p) + b_upd[...])
+    upd_bias = column(b_upd[...])
+    cand_bias = column(b_cand[...])
+    for p in range(9):
+        ph[0:96, p * 128:(p + 1) * 128] = jax.nn.sigmoid(shifted(pick(ph, 288), p) + upd_bias)
     rim_recv_all(2, gext)
     pe[0:288] = jnp.dot(wh[576:864], field(gext), preferred_element_type=F32) + pe[576:864]
     for p in range(9):
         z, y = p // 3, p % 3
-        cand = jnp.tanh(shifted(pick(pe, 0), p) + b_cand[...])
+        cand = jnp.tanh(shifted(pick(pe, 0), p) + cand_bias)
         u = ph[0:96, p * 128:(p + 1) * 128]
         new = ((1.0 - u) * hext[1 + z, 1 + y].astype(F32) + u * cand).astype(BF16)
         sext[1 + z, 1 + y] = new
@@ -362,7 +395,8 @@
     for p in range(9):
         z, y = p // 3, p % 3
         out = shifted([pe[c * 8:(c + 1) * 8] for c in range(3)], p)
-        motion_out[z, y] = motion[z, y] + out[0:3] + b_head[...]
+        for o in range(3):
+            motion_out[z, y, o:o + 1] = motion[z, y, o:o + 1] + out[o:o + 1] + b_head[0:1, o:o + 1]
 
     for k in range(3):
         partner_copy(k).wait_send()
@@ -403,8 +437,8 @@
                 pltpu.VMEM((864, 864), BF16), pltpu.VMEM((864, 864), BF16),
                 pltpu.VMEM((96, 896), BF16),
                 pltpu.VMEM((24, 864), BF16), pltpu.VMEM((24, 864), F32),
-                pltpu.VMEM((9, 128, 128), BF16),
-                pltpu.VMEM((63, 128, 128), BF16),
+                pltpu.VMEM((1152, 128), BF16),
+                pltpu.VMEM((1152, 896), BF16),
                 pltpu.VMEM((576, 1152), F32),
                 pltpu.VMEM((864, 1152), F32),
                 pltpu.SemaphoreType.DMA((6,)),
@@ -413,8 +447,8 @@
             ],
             compiler_params=pltpu.CompilerParams(
                 collective_id=0, has_side_effects=True, vmem_limit_bytes=60 * 2 ** 20),
-        )(source, target, hidden, motion, w_corr, w_motion, bias_encoder[:, None], w_update, bias_update[:, None], w_reset,
-          bias_reset[:, None], w_cand, bias_cand[:, None], w_head, bias_head[:, None])
+        )(source, target, hidden, motion, w_corr, w_motion.T, bias_encoder[None], w_update, bias_update[None], w_reset,
+          bias_reset[None], w_cand, bias_cand[None], w_head.transpose(1, 0, 2), bias_head[None])
 
     rows = P("gz", "gy", None, None)
     return jax.shard_map(

time: 113 us -> 67 us (0.59)
  the two profiles are of different devices: /device:TPU:463 before, /device:TPU:479 now
where the time goes in v1:
time: 67 us; the launch traced here: 66.7 us
  Pallas kernels  63.1 us (94%)
  local copies, waits for them, and re-layouts  2.97 us (4%)
    pallas_call x1, Pallas kernels, on_device(): pl.pallas_call(functools.partial(kernel, nz, ny), name='dvc_update', out_...  63.1 us
    unnamed x2, local copies, waits for them, and re-layouts  2.97 us

profile of v1, /device:TPU:479, one launch (start us, length us, event | category | flops | bytes accessed | tf_op | source)
XLA Modules:
  0.0 66.7 jit_solution(8618045259847293386)
XLA Ops:
  0.6 63.1 %dvc_update.1 = (bf16[3,3,96,128]{3,2,1,0:T(8,128)(2,1)}, f32[3,3,3,128]{3,2,1,0:T(4,128)}) custom-call(bf16[3,3,128,128]{3,2,1,0:T(8,128)(2,1)} %src_hbm.1, bf16[3,3,128,128]{3,2,1,0:T(8,128)(2,1)} %tgt_hbm.1, bf16[3,3,96,128]{3,2,1,0:T(8,128)(2,1)} %hid_hbm.1, f32[3,3,3,128]{3,2,1,0:T(4,128)} %motion.1, bf16[96,343]{1,0:T(8,128)(2,1)} %w_corr.1, ...), custom_call_target="tpu_custom_call" | custom-call | tf_op jit(solution)/shard_map/dvc_update/pallas_call | solution.py:425
  63.8 1.6 %copy.19 = bf16[3,3,96,128]{3,2,1,0:T(8,128)(2,1)} copy(bf16[3,3,96,128]{3,2,1,0:T(8,128)(2,1)} %get-tuple-element.4) | data formatting | bytes 442368
  65.4 1.3 %copy.20 = f32[3,3,3,128]{3,2,1,0:T(4,128)} copy(f32[3,3,3,128]{3,2,1,0:T(4,128)} %get-tuple-element.5) | data formatting | bytes 27648

commit v2 on v1

--- a/solution.py
+++ b/solution.py
@@ -10,7 +10,7 @@
 MESH = pl.DeviceIdType.MESH
 F32 = jnp.float32
 BF16 = jnp.bfloat16
-GROUPS = ((0, 1), (2, 3), (4, 5), (6, 7), (8,))
+GROUPS = tuple((r,) for r in range(9))
 DIRS = [(dz, dy) for dz in (-1, 0, 1) for dy in (-1, 0, 1) if (dz, dy) != (0, 0)]
 
 
@@ -21,7 +21,7 @@
 def kernel(nz, ny,
            src_hbm, tgt_hbm, hid_hbm, motion, w_corr, w_motion, b_enc, w_upd, b_upd, w_res, b_res, w_cand, b_cand, w_head, b_head,
            state_out, motion_out,
-           src, text, hext, eext, gext, sext, wraw, tmp_h, tmp_e, wh, we, wc, whead, headtmp, st, corr, ph, pe,
+           src, text, hext, eext, gext, sext, hsend, hrecv, wraw, tmp_h, tmp_e, wh, we, wc, whead, headtmp, st, corr, ph, pe,
            loc_sem, blk_send, blk_recv, rim_send, rim_recv):
     gz = lax.axis_index("gz")
     gy = lax.axis_index("gy")
@@ -58,6 +58,10 @@
         def _():
             pl.semaphore_signal(barrier, inc=1, device_id=(gz + dz, gy + dy), device_id_type=MESH)
 
+    for d, (dz, dy) in enumerate(DIRS):
+        @pl.when(jnp.logical_not(exists(-dz, -dy)))
+        def _():
+            hrecv[d] = jnp.zeros((3, 3, 8, 128), F32)
     for cond, at in (
         (gz == 0, (0, None)), (gz == nz - 1, (1, None)), (gy == 0, (None, 0)), (gy == ny - 1, (None, 1)),
     ):
@@ -68,7 +72,7 @@
                     text[6 * at[0] + i // 9, i % 9] = jnp.zeros((128, 128), BF16)
                     return c
                 lax.fori_loop(0, 27, zp, 0)
-                for e in (hext, eext, gext, sext):
+                for e in (hext, eext, gext):
                     def ze(i, c):
                         e[4 * at[0], i] = jnp.zeros((96, 128), BF16)
                         return c
@@ -78,11 +82,33 @@
                     text[i // 3, 6 * at[1] + i % 3] = jnp.zeros((128, 128), BF16)
                     return c
                 lax.fori_loop(0, 27, zp, 0)
-                for e in (hext, eext, gext, sext):
+                for e in (hext, eext, gext):
                     def ze(i, c):
                         e[i, 4 * at[1]] = jnp.zeros((96, 128), BF16)
                         return c
                     lax.fori_loop(0, 5, ze, 0)
+
+    lane8 = iota((8, 128), 1)
+    row8 = iota((8, 128), 0)
+    flip = jnp.where(iota((128, 128), 0) + iota((128, 128), 1) == 127, 1.0, 0.0).astype(BF16)
+
+    for a in range(7):
+        kk = iota((343, 128), 1)
+        want = a * 49 + (kk // 8) * 7 + kk % 8
+        pick = (iota((343, 128), 0) == want) & (kk % 8 < 7) & (kk < 56)
+        wc[:, a * 128:(a + 1) * 128] = jnp.dot(
+            w_corr[...], jnp.where(pick, 1.0, 0.0).astype(BF16), preferred_element_type=F32).astype(BF16)
+
+    local[1].wait()
+
+    for p in range(9):
+        st[p * 128:(p + 1) * 128] = lax.dot_general(
+            flip, src[p // 3, p % 3], (((1,), (1,)), ((), ())), preferred_element_type=F32).astype(BF16)
+
+    headtmp[...] = jnp.zeros_like(headtmp)
+    for o in range(3):
+        headtmp[pl.ds(o, 27, stride=8), :] = jnp.concatenate([w_head[o].astype(F32), jnp.zeros((27, 32), F32)], axis=1)
+    whead[...] = headtmp[...].astype(BF16)
 
     local[0].wait()
     local[2].wait()
@@ -144,7 +170,7 @@
             return pl.ds((3 if o > 0 else 1) if here else (0 if o > 0 else 4), 1)
         return pltpu.make_async_remote_copy(
             src_ref=ref.at[sl(dz, True), sl(dy, True)], dst_ref=ref.at[sl(dz, False), sl(dy, False)],
-            send_sem=rim_send.at[rnd * 8 + d], recv_sem=rim_recv.at[rnd * 8 + d],
+            send_sem=rim_send.at[rnd * 9 + d], recv_sem=rim_recv.at[rnd * 9 + d],
             device_id=(gz + dz, gy + dy), device_id_type=MESH)
 
     def rim_start(rnd, ref):
@@ -164,31 +190,6 @@
             @pl.when(exists(dz, dy))
             def _():
                 rim_copy(rnd, ref, d).wait_send()
-
-    lane8 = iota((8, 128), 1)
-    row8 = iota((8, 128), 0)
-    flip = jnp.where(iota((128, 128), 0) + iota((128, 128), 1) == 127, 1.0, 0.0).astype(BF16)
-
-    for a in range(7):
-        kk = iota((343, 128), 1)
-        want = a * 49 + (kk // 8) * 7 + kk % 8
-        pick = (iota((343, 128), 0) == want) & (kk % 8 < 7) & (kk < 56)
-        wc[:, a * 128:(a + 1) * 128] = jnp.dot(
-            w_corr[...], jnp.where(pick, 1.0, 0.0).astype(BF16), preferred_element_type=F32).astype(BF16)
-
-    local[1].wait()
-
-    for p in range(9):
-        st[p * 128:(p + 1) * 128] = lax.dot_general(
-            flip, src[p // 3, p % 3], (((1,), (1,)), ((), ())), preferred_element_type=F32).astype(BF16)
-
-    headtmp[...] = jnp.zeros_like(headtmp)
-    for o in range(3):
-        v = w_head[o].astype(F32)
-        for ab in range(9):
-            for c in range(3):
-                headtmp[c * 8 + o:c * 8 + o + 1, ab * 96:(ab + 1) * 96] = v[ab * 3 + c:ab * 3 + c + 1]
-    whead[...] = headtmp[...].astype(BF16)
 
     def spread(w):
         local[3 + w].wait()
@@ -288,57 +289,78 @@
         rows_recv(0, k)
 
     def own(i, c):
-        corr_rows(i // 3, 3 + i % 3)
-        for at, k in ((0, 0), (1, 1), (3, 2)):
-            @pl.when(i == at)
-            def _():
-                pass_relay(k)
+        for zt in (3, 4, 5):
+            corr_rows(i, zt)
+        pass_relay(i)
         return c
-    lax.fori_loop(0, 9, own, 0)
+    lax.fori_loop(0, 3, own, 0)
     rim_start(0, hext)
-
-    def side(n, carry):
-        up = (1 - odd) * (1 - n) + odd * n
-
-        @pl.when(n == 0)
-        def _():
-            for k in range(3):
-                rows_recv(1, k)
-
-        @pl.when((n == 1) & has_relay)
-        def _():
-            for k in range(3):
-                rows_recv(2, k)
-        for k in range(3):
-            def cell(z, c):
-                zt = 6 + k
-                corr_rows((1 - up) * (2 - z) + up * z, (1 - up) * (8 - zt) + up * zt)
-                return c
-            lax.fori_loop(k, 3, cell, 0)
-        return carry
-    lax.fori_loop(0, 2, side, 0)
 
     eye = iota((96, 96), 0) == iota((96, 96), 1)
 
     def column(row):
         return jnp.sum(jnp.where(eye, jnp.broadcast_to(row, (96, 96)), 0.0), axis=1, keepdims=True)
 
-    pe[0:96] = lax.dot_general(wc[...], corr[...], (((1,), (1,)), ((), ())), preferred_element_type=F32)
     back = 127 - lane8
-    enc_bias = jnp.broadcast_to(column(b_enc[...]), (96, 128))
-    enc_motion = [jnp.broadcast_to(column(w_motion[j:j + 1]), (96, 128)) for j in range(3)]
-    turned = []
-    for p in range(9):
-        m = motion[p // 3, p % 3]
-        e = pe[0:96, p * 128:(p + 1) * 128] + enc_bias
-        for j in range(3):
-            mj = jnp.take_along_axis(jnp.broadcast_to(m[j:j + 1], (8, 128)), back, axis=1, mode="promise_in_bounds")
-            e = e + enc_motion[j] * jnp.concatenate([mj] * 12, axis=0)
-        turned.append(jnp.maximum(e, 0.0).astype(BF16))
-    straight = jnp.dot(jnp.concatenate(turned, axis=0), flip, preferred_element_type=F32).astype(BF16)
-    for p in range(9):
-        eext[1 + p // 3, 1 + p % 3] = straight[p * 96:(p + 1) * 96]
-    rim_start(1, eext)
+
+    def encode(z):
+        acc = lax.dot_general(
+            wc[...], corr[pl.ds(pl.multiple_of(z * 384, 384), 384)], (((1,), (1,)), ((), ())), preferred_element_type=F32)
+        bias = column(b_enc[...])
+        turned = []
+        for y in range(3):
+            m = motion[z, y]
+            e = acc[:, y * 128:(y + 1) * 128] + bias
+            for j in range(3):
+                mj = jnp.take_along_axis(jnp.broadcast_to(m[j:j + 1], (8, 128)), back, axis=1, mode="promise_in_bounds")
+                e = e + column(w_motion[j:j + 1]) * jnp.concatenate([mj] * 12, axis=0)
+            turned.append(jnp.maximum(e, 0.0).astype(BF16))
+        straight = jnp.dot(jnp.concatenate(turned, axis=0), flip, preferred_element_type=F32).astype(BF16)
+        for y in range(3):
+            eext[1 + z, 1 + y] = straight[y * 96:(y + 1) * 96]
+
+    def e_rows(z, dy):
+        i = 36 + z * 2 + (dy + 1) // 2
+        return pltpu.make_async_remote_copy(
+            src_ref=eext.at[1 + z, 2 + dy], dst_ref=eext.at[1 + z, 2 - 2 * dy],
+            send_sem=rim_send.at[i], recv_sem=rim_recv.at[i], device_id=(gz, gy + dy), device_id_type=MESH)
+
+    def e_face(dz, dy):
+        i = 9 + (dz + 1) * 3 + dy + 1
+        here, there = (pl.ds(1, 3), pl.ds(1, 3)) if dy == 0 else (pl.ds(2 + dy, 1), pl.ds(2 - 2 * dy, 1))
+        return pltpu.make_async_remote_copy(
+            src_ref=eext.at[2 + dz, here], dst_ref=eext.at[2 - 2 * dz, there],
+            send_sem=rim_send.at[i], recv_sem=rim_recv.at[i], device_id=(gz + dz, gy + dy), device_id_type=MESH)
+
+    def when_exists(dz, dy, make, act):
+        @pl.when(exists(dz, dy))
+        def _():
+            getattr(make(), act)()
+
+    def side_tiles(up, zu):
+        z = (1 - up) * (2 - zu) + up * zu
+        for k in range(zu + 1):
+            corr_rows(z, (1 - up) * (2 - k) + up * (6 + k))
+        return z
+
+    for k in range(3):
+        rows_recv(1, k)
+    for zu in range(3):
+        side_tiles(1 - odd, zu)
+
+    @pl.when(has_relay)
+    def _():
+        for k in range(3):
+            rows_recv(2, k)
+    for zu in (2, 1, 0):
+        z = side_tiles(odd, zu)
+        encode(z)
+        for dy in (-1, 1):
+            when_exists(0, dy, lambda: e_rows(z, dy), "start")
+        if zu != 1:
+            dz = (zu - 1) * (2 * odd - 1)
+            for dy in (0, -1, 1):
+                when_exists(dz, dy, lambda: e_face(dz, dy), "start")
 
     def field(ref):
         cols = []
@@ -358,7 +380,12 @@
     collect(1)
     rim_recv_all(0, hext)
     ph[...] = jnp.dot(wh[0:576], field(hext), preferred_element_type=F32)
-    rim_recv_all(1, eext)
+    for dy in (-1, 1):
+        for z in range(3):
+            when_exists(0, -dy, lambda: e_rows(z, dy), "wait_recv")
+    for dz in (-1, 1):
+        for dy in (-1, 0, 1):
+            when_exists(-dz, -dy, lambda: e_face(dz, dy), "wait_recv")
     pe[0:288] = jnp.dot(we[0:288], field(eext), preferred_element_type=F32) + ph[0:288]
 
     def pick(ref, base):
@@ -387,14 +414,44 @@
         cand = jnp.tanh(shifted(pick(pe, 0), p) + cand_bias)
         u = ph[0:96, p * 128:(p + 1) * 128]
         new = ((1.0 - u) * hext[1 + z, 1 + y].astype(F32) + u * cand).astype(BF16)
-        sext[1 + z, 1 + y] = new
+        sext[:, p * 128:(p + 1) * 128] = new
         state_out[z, y] = new
-    rim_start(3, sext)
-    rim_recv_all(3, sext)
-    pe[0:24] = jnp.dot(whead[...], field(sext), preferred_element_type=F32)
+
+    pe[0:216] = jnp.dot(whead[:, 0:96], sext[...], preferred_element_type=F32)
+    for qz in (0, 4, 1, 2, 3):
+        for qy in range(5):
+            sums = [None] * 3
+            for a in range(3):
+                for b in range(3):
+                    z, y = qz + a - 2, qy + b - 2
+                    if 0 <= z < 3 and 0 <= y < 3:
+                        for c in range(3):
+                            row = ((a * 3 + b) * 3 + c) * 8
+                            v = pe[row:row + 8, (z * 3 + y) * 128:(z * 3 + y + 1) * 128]
+                            sums[c] = v if sums[c] is None else sums[c] + v
+            left = jnp.where(lane8 == 0, 0.0, pltpu.roll(sums[0], 1, 1))
+            right = jnp.where(lane8 == 127, 0.0, pltpu.roll(sums[2], 127, 1))
+            hsend[qz, qy] = left + sums[1] + right
+
+    def head_copy(d):
+        dz, dy = DIRS[d]
+        here = [pl.ds(1, 3) if o == 0 else pl.ds(2 + 2 * o, 1) for o in (dz, dy)]
+        there = [pl.ds(0, 3) if o == 0 else pl.ds(1 - o, 1) for o in (dz, dy)]
+        return pltpu.make_async_remote_copy(
+            src_ref=hsend.at[here[0], here[1]], dst_ref=hrecv.at[d, there[0], there[1]],
+            send_sem=rim_send.at[27 + d], recv_sem=rim_recv.at[27 + d],
+            device_id=(gz + dz, gy + dy), device_id_type=MESH)
+
+    for d, (dz, dy) in enumerate(DIRS):
+        when_exists(dz, dy, lambda: head_copy(d), "start")
+    for d, (dz, dy) in enumerate(DIRS):
+        when_exists(-dz, -dy, lambda: head_copy(d), "wait_recv")
     for p in range(9):
         z, y = p // 3, p % 3
-        out = shifted([pe[c * 8:(c + 1) * 8] for c in range(3)], p)
+        out = hsend[1 + z, 1 + y]
+        for d, (dz, dy) in enumerate(DIRS):
+            if (dz == 0 or z == 1 - dz) and (dy == 0 or y == 1 - dy):
+                out = out + hrecv[d, z, y]
         for o in range(3):
             motion_out[z, y, o:o + 1] = motion[z, y, o:o + 1] + out[o:o + 1] + b_head[0:1, o:o + 1]
 
@@ -410,8 +467,21 @@
         @pl.when(has_relay)
         def _():
             rows_sent(2, k)
-    for rnd, ref in enumerate((hext, eext, gext, sext)):
+    for rnd, ref in ((0, hext), (2, gext)):
         rim_sent(rnd, ref)
+    for dy in (-1, 1):
+        for z in range(3):
+            when_exists(0, dy, lambda: e_rows(z, dy), "wait_send")
+    for dz in (-1, 1):
+        for dy in (-1, 0, 1):
+            when_exists(dz, dy, lambda: e_face(dz, dy), "wait_send")
+    for d, (dz, dy) in enumerate(DIRS):
+        when_exists(dz, dy, lambda: head_copy(d), "wait_send")
+
+
+def hand_on(a, b, c, d):
+    c[...] = a[...]
+    d[...] = b[...]
 
 
 def solution(mesh):
@@ -422,7 +492,7 @@
         hbm = pl.BlockSpec(memory_space=pl.ANY)
         vmem = pl.BlockSpec(memory_space=pltpu.VMEM)
         ext = pltpu.VMEM((5, 5, 96, 128), BF16)
-        return pl.pallas_call(
+        made = pl.pallas_call(
             functools.partial(kernel, nz, ny),
             name="dvc_update",
             out_shape=(jax.ShapeDtypeStruct((3, 3, 96, 128), BF16), jax.ShapeDtypeStruct((3, 3, 3, 128), F32)),
@@ -431,24 +501,31 @@
             scratch_shapes=[
                 pltpu.VMEM((3, 3, 128, 128), BF16),
                 pltpu.VMEM((9, 9, 128, 128), BF16),
-                ext, ext, ext, ext,
+                ext, ext, ext,
+                pltpu.VMEM((96, 1152), BF16),
+                pltpu.VMEM((5, 5, 8, 128), F32), pltpu.VMEM((8, 3, 3, 8, 128), F32),
                 pltpu.VMEM((3, 27, 18432), BF16),
                 pltpu.VMEM((3072, 128), F32), pltpu.VMEM((3072, 128), F32),
                 pltpu.VMEM((864, 864), BF16), pltpu.VMEM((864, 864), BF16),
                 pltpu.VMEM((96, 896), BF16),
-                pltpu.VMEM((24, 864), BF16), pltpu.VMEM((24, 864), F32),
+                pltpu.VMEM((216, 128), BF16), pltpu.VMEM((216, 128), F32),
                 pltpu.VMEM((1152, 128), BF16),
                 pltpu.VMEM((1152, 896), BF16),
                 pltpu.VMEM((576, 1152), F32),
                 pltpu.VMEM((864, 1152), F32),
                 pltpu.SemaphoreType.DMA((6,)),
                 pltpu.SemaphoreType.DMA((24,)), pltpu.SemaphoreType.DMA((24,)),
-                pltpu.SemaphoreType.DMA((32,)), pltpu.SemaphoreType.DMA((32,)),
+                pltpu.SemaphoreType.DMA((42,)), pltpu.SemaphoreType.DMA((42,)),
             ],
             compiler_params=pltpu.CompilerParams(
                 collective_id=0, has_side_effects=True, vmem_limit_bytes=60 * 2 ** 20),
         )(source, target, hidden, motion, w_corr, w_motion.T, bias_encoder[None], w_update, bias_update[None], w_reset,
           bias_reset[None], w_cand, bias_cand[None], w_head.transpose(1, 0, 2), bias_head[None])
+        return pl.pallas_call(
+            hand_on, name="hand_on",
+            out_shape=(jax.ShapeDtypeStruct((3, 3, 96, 128), BF16), jax.ShapeDtypeStruct((3, 3, 3, 128), F32)),
+            in_specs=[vmem, vmem], out_specs=(vmem, vmem),
+        )(*made)
 
     rows = P("gz", "gy", None, None)
     return jax.shard_map(

time: 67 us -> 58 us (0.87)
  the two profiles are of different devices: /device:TPU:479 before, /device:TPU:22 now
where the time goes in v2:
time: 58 us; the launch traced here: 57.8 us
  Pallas kernels  57.2 us (99%)
  between operations  0.64 us (1%)
    pallas_call x1, Pallas kernels, on_device(): pl.pallas_call(functools.partial(kernel, nz, ny), name='dvc_update', out_...  55.5 us
    pallas_call x1, Pallas kernels, on_device(): pl.pallas_call(hand_on, name='hand_on', out_shape=(jax.ShapeDtypeStruct((...  1.64 us

profile of v2, /device:TPU:22, one launch (start us, length us, event | category | flops | bytes accessed | tf_op | source)
XLA Modules:
  0.0 57.8 jit_solution(12650350852266063043)
XLA Ops:
  0.6 55.5 %dvc_update.1 = (bf16[3,3,96,128]{3,2,1,0:T(8,128)(2,1)}, f32[3,3,3,128]{3,2,1,0:T(4,128)}) custom-call(bf16[3,3,128,128]{3,2,1,0:T(8,128)(2,1)} %src_hbm.1, bf16[3,3,128,128]{3,2,1,0:T(8,128)(2,1)} %tgt_hbm.1, bf16[3,3,96,128]{3,2,1,0:T(8,128)(2,1)} %hid_hbm.1, f32[3,3,3,128]{3,2,1,0:T(4,128)} %motion.1, bf16[96,343]{1,0:T(8,128)(2,1)} %w_corr.1, ...), custom_call_target="tpu_custom_call" | custom-call | tf_op jit(solution)/shard_map/dvc_update/pallas_call | solution.py:495
  56.2 1.6 %hand_on.1 = (bf16[3,3,96,128]{3,2,1,0:T(8,128)(2,1)}, f32[3,3,3,128]{3,2,1,0:T(4,128)}) custom-call(bf16[3,3,96,128]{3,2,1,0:T(8,128)(2,1)} %get-tuple-element.4.a, f32[3,3,3,128]{3,2,1,0:T(4,128)} %get-tuple-element.5.b), custom_call_target="tpu_custom_call" | custom-call | tf_op jit(solution)/shard_map/hand_on/pallas_call | solution.py:524

commit v3 on v2

--- a/solution.py
+++ b/solution.py
@@ -138,22 +138,41 @@
             device_id=(gz, gy + 2 * side - 1), device_id_type=MESH)
 
     side_ok = (gy > 0, gy < ny - 1)
+    mid = ny // 2
+    cross = (gy == mid, gy == mid - 1)
+    at_cross = cross[0] | cross[1]
+    far = 6 * (mid - gy)
+
+    def open_side(group, side):
+        return side_ok[side] if group == 0 else side_ok[side] & jnp.logical_not(cross[side])
+
+    def far_partner(k):
+        return pltpu.make_async_remote_copy(
+            src_ref=text.at[3 + k, pl.ds(far, 3)], dst_ref=text.at[relay_plane + k, pl.ds(far, 3)],
+            send_sem=blk_send.at[24 + k], recv_sem=blk_recv.at[24 + k],
+            device_id=(gz + s, gy), device_id_type=MESH)
+
+    def far_relay(k):
+        return pltpu.make_async_remote_copy(
+            src_ref=text.at[part_plane + k, pl.ds(far, 3)], dst_ref=text.at[relay_plane + k, pl.ds(far, 3)],
+            send_sem=blk_send.at[27 + k], recv_sem=blk_recv.at[27 + k],
+            device_id=(gz + 2 * s, gy), device_id_type=MESH)
 
     def rows_start(group, k):
         for side in (0, 1):
-            @pl.when(side_ok[side])
+            @pl.when(open_side(group, side))
             def _():
                 row_copy(group, k, side).start()
 
     def rows_recv(group, k):
         for side in (0, 1):
-            @pl.when(side_ok[1 - side])
+            @pl.when(open_side(group, 1 - side))
             def _():
                 row_copy(group, k, side).wait_recv()
 
     def rows_sent(group, k):
         for side in (0, 1):
-            @pl.when(side_ok[side])
+            @pl.when(open_side(group, side))
             def _():
                 row_copy(group, k, side).wait_send()
 
@@ -228,10 +247,10 @@
             relay_copy(k).wait_recv()
             rows_start(2, k)
 
+    spread(0)
     pass_partner(0)
-    spread(0)
+    collect(0)
     pass_partner(1)
-    collect(0)
     pass_partner(2)
 
     half = lane8 < 64
@@ -288,10 +307,22 @@
     for k in range(3):
         rows_recv(0, k)
 
+        @pl.when(at_cross)
+        def _():
+            far_partner(k).start()
+
     def own(i, c):
         for zt in (3, 4, 5):
             corr_rows(i, zt)
         pass_relay(i)
+
+        @pl.when(at_cross)
+        def _():
+            far_partner(i).wait_recv()
+
+            @pl.when(has_relay_dst)
+            def _():
+                far_relay(i).start()
         return c
     lax.fori_loop(0, 3, own, 0)
     rim_start(0, hext)
@@ -352,6 +383,10 @@
     def _():
         for k in range(3):
             rows_recv(2, k)
+
+            @pl.when(at_cross)
+            def _():
+                far_relay(k).wait_recv()
     for zu in (2, 1, 0):
         z = side_tiles(odd, zu)
         encode(z)
@@ -467,6 +502,14 @@
         @pl.when(has_relay)
         def _():
             rows_sent(2, k)
+
+        @pl.when(at_cross)
+        def _():
+            far_partner(k).wait_send()
+
+            @pl.when(has_relay_dst)
+            def _():
+                far_relay(k).wait_send()
     for rnd, ref in ((0, hext), (2, gext)):
         rim_sent(rnd, ref)
     for dy in (-1, 1):
@@ -514,7 +557,7 @@
                 pltpu.VMEM((576, 1152), F32),
                 pltpu.VMEM((864, 1152), F32),
                 pltpu.SemaphoreType.DMA((6,)),
-                pltpu.SemaphoreType.DMA((24,)), pltpu.SemaphoreType.DMA((24,)),
+                pltpu.SemaphoreType.DMA((30,)), pltpu.SemaphoreType.DMA((30,)),
                 pltpu.SemaphoreType.DMA((42,)), pltpu.SemaphoreType.DMA((42,)),
             ],
             compiler_params=pltpu.CompilerParams(

time: 58 us -> 56.5 us (0.974)
  the two profiles are of different devices: /device:TPU:22 before, /device:TPU:14 now
where the time goes in v3:
time: 56.5 us; the launch traced here: 56.3 us
  Pallas kernels  55.7 us (99%)
  between operations  0.64 us (1%)
    pallas_call x1, Pallas kernels, on_device(): pl.pallas_call(functools.partial(kernel, nz, ny), name='dvc_update', out_...  54 us
    pallas_call x1, Pallas kernels, on_device(): pl.pallas_call(hand_on, name='hand_on', out_shape=(jax.ShapeDtypeStruct((...  1.64 us

profile of v3, /device:TPU:14, one launch (start us, length us, event | category | flops | bytes accessed | tf_op | source)
XLA Modules:
  0.0 56.3 jit_solution(7270009683662286756)
XLA Ops:
  0.6 54.0 %dvc_update.1 = (bf16[3,3,96,128]{3,2,1,0:T(8,128)(2,1)}, f32[3,3,3,128]{3,2,1,0:T(4,128)}) custom-call(bf16[3,3,128,128]{3,2,1,0:T(8,128)(2,1)} %src_hbm.1, bf16[3,3,128,128]{3,2,1,0:T(8,128)(2,1)} %tgt_hbm.1, bf16[3,3,96,128]{3,2,1,0:T(8,128)(2,1)} %hid_hbm.1, f32[3,3,3,128]{3,2,1,0:T(4,128)} %motion.1, bf16[96,343]{1,0:T(8,128)(2,1)} %w_corr.1, ...), custom_call_target="tpu_custom_call" | custom-call | tf_op jit(solution)/shard_map/dvc_update/pallas_call | solution.py:538
  54.7 1.6 %hand_on.1 = (bf16[3,3,96,128]{3,2,1,0:T(8,128)(2,1)}, f32[3,3,3,128]{3,2,1,0:T(4,128)}) custom-call(bf16[3,3,96,128]{3,2,1,0:T(8,128)(2,1)} %get-tuple-element.4.a, f32[3,3,3,128]{3,2,1,0:T(4,128)} %get-tuple-element.5.b), custom_call_target="tpu_custom_call" | custom-call | tf_op jit(solution)/shard_map/hand_on/pallas_call | solution.py:567

commit v4 on v3

--- a/solution.py
+++ b/solution.py
@@ -251,6 +251,7 @@
     pass_partner(0)
     collect(0)
     pass_partner(1)
+    spread(1)
     pass_partner(2)
 
     half = lane8 < 64
@@ -378,6 +379,7 @@
         rows_recv(1, k)
     for zu in range(3):
         side_tiles(1 - odd, zu)
+    collect(1)
 
     @pl.when(has_relay)
     def _():
@@ -411,8 +413,6 @@
         right = jnp.where(lane == 127, 0.0, pltpu.roll(parts[2][:, cut], 127, 1))
         return left + parts[1][:, cut] + right
 
-    spread(1)
-    collect(1)
     rim_recv_all(0, hext)
     ph[...] = jnp.dot(wh[0:576], field(hext), preferred_element_type=F32)
     for dy in (-1, 1):
@@ -452,6 +452,15 @@
         sext[:, p * 128:(p + 1) * 128] = new
         state_out[z, y] = new
 
+    def head_copy(d):
+        dz, dy = DIRS[d]
+        here = [pl.ds(1, 3) if o == 0 else pl.ds(2 + 2 * o, 1) for o in (dz, dy)]
+        there = [pl.ds(0, 3) if o == 0 else pl.ds(1 - o, 1) for o in (dz, dy)]
+        return pltpu.make_async_remote_copy(
+            src_ref=hsend.at[here[0], here[1]], dst_ref=hrecv.at[d, there[0], there[1]],
+            send_sem=rim_send.at[27 + d], recv_sem=rim_recv.at[27 + d],
+            device_id=(gz + dz, gy + dy), device_id_type=MESH)
+
     pe[0:216] = jnp.dot(whead[:, 0:96], sext[...], preferred_element_type=F32)
     for qz in (0, 4, 1, 2, 3):
         for qy in range(5):
@@ -467,18 +476,14 @@
             left = jnp.where(lane8 == 0, 0.0, pltpu.roll(sums[0], 1, 1))
             right = jnp.where(lane8 == 127, 0.0, pltpu.roll(sums[2], 127, 1))
             hsend[qz, qy] = left + sums[1] + right
-
-    def head_copy(d):
-        dz, dy = DIRS[d]
-        here = [pl.ds(1, 3) if o == 0 else pl.ds(2 + 2 * o, 1) for o in (dz, dy)]
-        there = [pl.ds(0, 3) if o == 0 else pl.ds(1 - o, 1) for o in (dz, dy)]
-        return pltpu.make_async_remote_copy(
-            src_ref=hsend.at[here[0], here[1]], dst_ref=hrecv.at[d, there[0], there[1]],
-            send_sem=rim_send.at[27 + d], recv_sem=rim_recv.at[27 + d],
-            device_id=(gz + dz, gy + dy), device_id_type=MESH)
+        if qz in (0, 4):
+            for d, (dz, dy) in enumerate(DIRS):
+                if dz == (qz - 2) // 2:
+                    when_exists(dz, dy, lambda: head_copy(d), "start")
 
     for d, (dz, dy) in enumerate(DIRS):
-        when_exists(dz, dy, lambda: head_copy(d), "start")
+        if dz == 0:
+            when_exists(dz, dy, lambda: head_copy(d), "start")
     for d, (dz, dy) in enumerate(DIRS):
         when_exists(-dz, -dy, lambda: head_copy(d), "wait_recv")
     for p in range(9):

time: 56.5 us -> 55.2 us (0.977)
  the two profiles are of different devices: /device:TPU:14 before, /device:TPU:30 now
where the time goes in v4:
time: 55.2 us; the launch traced here: 55 us
  Pallas kernels  54.3 us (98%)
  between operations  0.64 us (1%)
    pallas_call x1, Pallas kernels, on_device(): pl.pallas_call(functools.partial(kernel, nz, ny), name='dvc_update', out_...  52.7 us
    pallas_call x1, Pallas kernels, on_device(): pl.pallas_call(hand_on, name='hand_on', out_shape=(jax.ShapeDtypeStruct((...  1.64 us

profile of v4, /device:TPU:30, one launch (start us, length us, event | category | flops | bytes accessed | tf_op | source)
XLA Modules:
  0.0 55.0 jit_solution(15458079021746637199)
XLA Ops:
  0.6 52.7 %dvc_update.1 = (bf16[3,3,96,128]{3,2,1,0:T(8,128)(2,1)}, f32[3,3,3,128]{3,2,1,0:T(4,128)}) custom-call(bf16[3,3,128,128]{3,2,1,0:T(8,128)(2,1)} %src_hbm.1, bf16[3,3,128,128]{3,2,1,0:T(8,128)(2,1)} %tgt_hbm.1, bf16[3,3,96,128]{3,2,1,0:T(8,128)(2,1)} %hid_hbm.1, f32[3,3,3,128]{3,2,1,0:T(4,128)} %motion.1, bf16[96,343]{1,0:T(8,128)(2,1)} %w_corr.1, ...), custom_call_target="tpu_custom_call" | custom-call | tf_op jit(solution)/shard_map/dvc_update/pallas_call | solution.py:543
  53.3 1.6 %hand_on.1 = (bf16[3,3,96,128]{3,2,1,0:T(8,128)(2,1)}, f32[3,3,3,128]{3,2,1,0:T(4,128)}) custom-call(bf16[3,3,96,128]{3,2,1,0:T(8,128)(2,1)} %get-tuple-element.4.a, f32[3,3,3,128]{3,2,1,0:T(4,128)} %get-tuple-element.5.b), custom_call_target="tpu_custom_call" | custom-call | tf_op jit(solution)/shard_map/hand_on/pallas_call | solution.py:572
